TPU v7x, 512 devices: a whole 4x8x8 slice. The times are simulated.
512 devices in a mesh: dp: 128 (over y, z, core), mp: 4 (over x).
Axes of the slice: x: 4, y: 8, z: 8, core: 2. Of those that a mesh axis runs over, the one named last changes fastest.
Arguments:
- frames: bfloat16 [32768, 1024], P('dp'), may hold values from -24 to 24
- proj_in: bfloat16 [1024, 2, 1024], P(None, None, 'mp'), may hold values from -0.1875 to 0.1875
- depthwise: float32 [31, 1024], P(None, 'mp'), may hold values from -1 to 1
- bn_gain: float32 [1024], P('mp'), may hold values from 0.5 to 1.5
- bn_shift: float32 [1024], P('mp'), may hold values from -3 to 3
- proj_out: bfloat16 [1024, 1024], P(None, 'mp'), may hold values from -0.1875 to 0.1875
- grad_out: bfloat16 [32768, 1024], P('dp'), may hold values from -24 to 24
- counts: int32 [128], replicated, may hold values from 1 to 2, as said below
- lengths: int32 [128, 2], P('dp'), may hold values from 1 to 255, as said below
Outputs:
- frame_grad: bfloat16 [32768, 1024], P('dp', 'mp')
- in_grad: float32 [1024, 2, 1024], P('dp', None, 'mp')
- out_grad: float32 [1024, 1024], P('dp', 'mp')
- depth_grad: float32 [31, 1024], P(None, 'mp')
- gain_grad: float32 [1024], P('mp')
- shift_grad: float32 [1024], P('mp')
Inputs may be any that keep to these rules, and one draw needn't show every extreme that they name: `counts`: some device holds 2 live blocks. lengths[d] sums to 128 * counts[d]; on some device with 2 live blocks one utterance holds all frames but one for each other utterance.
All inputs are finite; a program needn't handle non-finite values.
Results may differ from a plain program's by a relative error of at most 0.0095.
Values may be sent and summed in bfloat16 or wider, within the bound.
No kernel may reach another device: no remote copies, remote signals or barrier semaphores. Data moves between devices by JAX's collectives and lax.ppermute only.
A program may use at most 64 MiB of HBM per device.

v0:
```python
import jax
import jax.numpy as jnp
from jax import lax
from jax.sharding import Mesh, PartitionSpec as P

BLOCK = 128
DP = ("y", "z", "core")


def time_shift(values, offset, fill_value):
    if offset > 0:
        pad_part = jnp.full((offset,) + values.shape[1:], fill_value, values.dtype)
        return jnp.concatenate([values[offset:], pad_part], axis=0)
    if offset < 0:
        pad_part = jnp.full((-offset,) + values.shape[1:], fill_value, values.dtype)
        return jnp.concatenate([pad_part, values[:offset]], axis=0)
    return values


def tap_term(glu_float, owner_id, live_col, offset):
    same_utt = (time_shift(owner_id, offset, -1) == owner_id).astype(jnp.float32)[
        :, None
    ] * live_col
    return time_shift(glu_float, offset, 0.0) * same_utt


def small_sum(x):
    x = lax.psum(x, "core")
    peers = lax.axis_size("y") * lax.axis_size("z")
    every = jnp.broadcast_to(x[None], (peers,) + x.shape)
    return jnp.sum(lax.all_to_all(every, ("y", "z"), 0, 0), axis=0)


def scatter_sum(partial):
    peers = lax.axis_size("y") * lax.axis_size("z")
    rows = partial.shape[0] // (2 * peers)
    parts = partial.reshape(peers, 2, rows, partial.shape[1])
    core = lax.axis_index("core")
    keep = lax.dynamic_index_in_dim(parts, core, 1, keepdims=False)
    send = lax.dynamic_index_in_dim(parts, 1 - core, 1, keepdims=False).astype(jnp.bfloat16)
    got = lax.ppermute(send, "core", [(0, 1), (1, 0)])
    both = (keep + got.astype(jnp.float32)).astype(jnp.bfloat16)
    every = lax.all_to_all(both, ("y", "z"), 0, 0)
    return jnp.sum(every.astype(jnp.float32), axis=0)


def shards(frames, proj_in, depthwise, bn_gain, bn_shift, proj_out, grad_out, counts, lengths):
    frames_dev = frames.shape[0]
    model_width = frames.shape[1]
    channels = proj_in.shape[2]
    tap_count = depthwise.shape[0]
    radius = tap_count // 2
    rows_dev = model_width // lax.axis_size(DP)
    groups = lax.axis_size("mp")
    position = jnp.arange(frames_dev, dtype=jnp.int32)
    utt_ends = jnp.cumsum(lengths[0])
    owner_id = jnp.sum((position[:, None] >= utt_ends[None, :]).astype(jnp.int32), axis=1)
    my_count = counts[lax.axis_index(DP)]
    live_col = (position < my_count * BLOCK).astype(jnp.float32)[:, None]
    frame_total = (jnp.sum(counts) * BLOCK).astype(jnp.float32)
    proj_flat = proj_in.reshape(model_width, 2 * channels)
    pre_act = jnp.dot(frames, proj_flat, preferred_element_type=jnp.float32)
    value_half = pre_act[:, :channels]
    gate_sig = jax.nn.sigmoid(pre_act[:, channels:])
    glu_out = (value_half * gate_sig * live_col).astype(jnp.bfloat16)
    glu_float = lax.optimization_barrier(glu_out).astype(jnp.float32)
    conv_out = jnp.zeros((frames_dev, channels), jnp.float32)
    for tap_index in range(tap_count):
        conv_out = conv_out + depthwise[tap_index] * tap_term(
            glu_float, owner_id, live_col, tap_index - radius
        )
    sum_val, sum_sq = small_sum(
        jnp.stack([jnp.sum(conv_out, axis=0), jnp.sum(conv_out * conv_out, axis=0)])
    )
    mean_val = sum_val / frame_total
    square_mean = sum_sq / frame_total
    inv_std = lax.rsqrt(square_mean - mean_val * mean_val + 1e-05)
    normed = (conv_out - mean_val) * inv_std
    scaled = normed * bn_gain + bn_shift
    sig_scaled = jax.nn.sigmoid(scaled)
    hidden = (scaled * sig_scaled * live_col).astype(jnp.bfloat16)
    grad_hidden = jnp.dot(grad_out, proj_out, preferred_element_type=jnp.float32) * live_col
    grad_scaled = grad_hidden * sig_scaled * (1.0 + scaled * (1.0 - sig_scaled))
    local_shift = jnp.sum(grad_scaled, axis=0)
    local_gain = jnp.sum(grad_scaled * normed, axis=0)
    shift_grad, gain_grad = small_sum(jnp.stack([local_shift, local_gain]))
    grad_conv = (
        live_col
        * bn_gain
        * inv_std
        * (grad_scaled - shift_grad / frame_total - normed * gain_grad / frame_total)
    )
    depth_rows = []
    for tap_index in range(tap_count):
        depth_rows.append(
            jnp.sum(grad_conv * tap_term(glu_float, owner_id, live_col, tap_index - radius), axis=0)
        )
    depth_grad = lax.psum(lax.psum(lax.psum(jnp.stack(depth_rows), "core"), "y"), "z")
    grad_glu = jnp.zeros((frames_dev, channels), jnp.float32)
    for tap_index in range(tap_count):
        offset = tap_index - radius
        back_same = (time_shift(owner_id, -offset, -1) == owner_id).astype(jnp.float32)[
            :, None
        ] * live_col
        grad_glu = grad_glu + depthwise[tap_index] * time_shift(grad_conv, -offset, 0.0) * back_same
    grad_value = grad_glu * gate_sig
    grad_gate = grad_glu * value_half * gate_sig * (1.0 - gate_sig)
    grad_flat = jnp.concatenate([grad_value, grad_gate], axis=1).astype(jnp.bfloat16)
    frame_term = lax.dot_general(
        proj_flat, grad_flat, (((1,), (1,)), ((), ())), preferred_element_type=jnp.float32
    ).T.astype(jnp.bfloat16)
    frame_parts = frame_term.reshape(frames_dev, groups, model_width // groups)
    frame_parts = lax.all_to_all(jnp.swapaxes(frame_parts, 0, 1), "mp", 0, 0)
    frame_grad = jnp.sum(frame_parts.astype(jnp.float32), axis=0).astype(jnp.bfloat16)
    summed = scatter_sum(
        jnp.concatenate(
            [
                lax.dot_general(
                    frames, grad_flat, (((0,), (0,)), ((), ())), preferred_element_type=jnp.float32
                ),
                lax.dot_general(
                    grad_out, hidden, (((0,), (0,)), ((), ())), preferred_element_type=jnp.float32
                ),
            ],
            axis=1,
        )
    )
    in_flat = summed[:, : 2 * channels]
    out_grad = summed[:, 2 * channels :]
    in_grad = in_flat.reshape(rows_dev, 2, channels)
    return (frame_grad, in_grad, out_grad, depth_grad, gain_grad, shift_grad)


def solution(mesh):
    grid = Mesh(mesh.devices.reshape(8, 8, 2, 4), ("y", "z", "core", "mp"))
    placed = (
        P(DP, None),
        P(None, None, "mp"),
        P(None, "mp"),
        P("mp"),
        P("mp"),
        P(None, "mp"),
        P(DP, None),
        P(),
        P(DP, None),
    )
    return jax.shard_map(
        shards,
        mesh=grid,
        in_specs=placed,
        out_specs=(P(DP, "mp"), P(DP, None, "mp"), P(DP, "mp"), P(None, "mp"), P("mp"), P("mp")),
        check_vma=False,
    )
```

profile of v0, /device:TPU:2, one launch (start us, length us, event | category | flops | bytes accessed | tf_op | source)
XLA Modules:
  0.0 197.2 jit_solution(1703413751848722447)
XLA Ops:
  4.6 1.5 copy.31
  11.3 3.9 %fusion.49 = (f32[256]{0:T(256)S(1)}, f32[256]{0:T(256)S(1)}, f32[256,256]{1,0:T(8,128)S(1)}) fusion(f32[256]{0:T(256)S(1)} %get-tuple-element.142, f32[241,256]{1,0:T(8,128)S(1)} %get-tuple-element.78, f32[256]{0:T(256)} %bitcast.33, f32[256]{0:T(256)S(1)} %get-tuple-element.143, f32[242,256]{1,0:T(8,128)S(1)} %get-tuple-element.80, f32[256]{0:T(256)} %bitcast.32, ...), kind=kLoop, calls=%fused_computation.171 | loop fusion | flops 6290944 | bytes 8077312 | tf_op jit(solution)/shard_map/reduce_sum | solution.py:73
  16.1 3.1 %psum.35 = f32[2,256]{1,0:T(2,128)} all-reduce(f32[2,256]{1,0:T(2,128)} %pad_maximum_fusion.4), channel_id=1, replica_groups=mesh['y'=8,'z'=8,'core'=2,'mp'=4] {'core'}, use_global_device_ids=true, to_apply=%region_4.5 | all-reduce | flops 512 | bytes 4096 | tf_op jit(solution)/shard_map/psum | solution.py:28
  19.2 1.4 broadcast_in_dim.4
  20.6 16.8 %all-to-all-start = ((f32[64,2,256]{2,1,0:T(2,128)}), f32[64,2,256]{2,1,0:T(2,128)}, u32[]{:S(2)}, u32[]{:S(2)}) async-start(f32[64,2,256]{2,1,0:T(2,128)} %broadcast_in_dim.4), calls=%async_computation | async-start | bytes 262144 | tf_op jit(solution)/shard_map/all_to_all | solution.py:31
  39.4 10.9 %all-to-all-done = f32[64,2,256]{2,1,0:T(2,128)} async-done(((f32[64,2,256]{2,1,0:T(2,128)}), f32[64,2,256]{2,1,0:T(2,128)}, u32[]{:S(2)}, u32[]{:S(2)}) %all-to-all-start) | async-done | bytes 131104 | tf_op jit(solution)/shard_map/all_to_all | solution.py:31
  50.3 1.6 reduce_sum.375
  53.2 2.2 %fusion.48 = (f32[256]{0:T(256)S(1)}, f32[256]{0:T(256)S(1)}, f32[256,256]{1,0:T(8,128)}) fusion(f32[256]{0:T(256)S(1)} %bitcast.118, f32[256,256]{1,0:T(8,128)S(1)} %get-tuple-element.46, f32[256]{0:T(256)S(1)} %bitcast.121, f32[256]{0:T(256)} %param.13, f32[256]{0:T(256)} %param.12, f32[256]{0:T(256)S(1)} %fusion.44, bf16[256,1024]{1,0:T(8,128)(2,1)} %param.15, ...), kind=kOutput, calls=%fused_computation.170 | convolution fusion | flops 135265792 | bytes 1580032 | tf_op jit(solution)/shard_map/dot_general | solution.py:82
  56.0 3.1 %psum.36 = f32[2,256]{1,0:T(2,128)} all-reduce(f32[2,256]{1,0:T(2,128)} %pad_maximum_fusion.5), channel_id=1, replica_groups=mesh['y'=8,'z'=8,'core'=2,'mp'=4] {'core'}, use_global_device_ids=true, to_apply=%region_9.10 | all-reduce | flops 512 | bytes 4096 | tf_op jit(solution)/shard_map/psum | solution.py:28
  59.2 1.4 broadcast_in_dim.5
  60.5 5.4 %all-to-all-start.1 = ((f32[64,2,256]{2,1,0:T(2,128)}), f32[64,2,256]{2,1,0:T(2,128)}, u32[]{:S(2)}, u32[]{:S(2)}) async-start(f32[64,2,256]{2,1,0:T(2,128)} %broadcast_in_dim.5), calls=%async_computation.1 | async-start | bytes 262144 | tf_op jit(solution)/shard_map/all_to_all | solution.py:31
  66.0 2.5 %convolution_bitcast_fusion.1 = f32[1024,256]{0,1:T(8,128)} fusion(bf16[256,1024]{1,0:T(8,128)(2,1)} %param.15, f32[256,256]{1,0:T(8,128)S(1)} %get-tuple-element.46, f32[256]{0:T(256)} %param.13, f32[256]{0:T(256)} %bitcast.122, f32[256]{0:T(256)} %bitcast.119, f32[256]{0:T(256)} %param.12, f32[256]{0:T(256)S(1)} %fusion.44), kind=kOutput, calls=%fused_computation.6 | convolution fusion | flops 134873088 | bytes 1840128 | tf_op jit(solution)/shard_map/dot_general | solution.py:121
  68.5 10.7 %all-to-all-done.1 = f32[64,2,256]{2,1,0:T(2,128)} async-done(((f32[64,2,256]{2,1,0:T(2,128)}), f32[64,2,256]{2,1,0:T(2,128)}, u32[]{:S(2)}, u32[]{:S(2)}) %all-to-all-start.1) | async-done | bytes 131104 | tf_op jit(solution)/shard_map/all_to_all | solution.py:31
  79.2 1.6 reduce_sum.379
  80.7 1.3 fusion.82
  82.1 2.9 %multiply_reduce_fusion = (f32[256]{0:T(256)}, f32[256]{0:T(256)}, f32[256]{0:T(256)}, f32[256]{0:T(256)}, f32[256]{0:T(256)}, /*index=5*/f32[256]{0:T(256)}, f3...) fusion(f32[241,256]{1,0:T(8,128)} %copy-done.28, f32[256]{0:T(256)S(1)} %get-tuple-element.142, ...), kind=kLoop, calls=%fused_computation.18 | loop fusion | flops 2356992 | bytes 3068932 | tf_op jit(solution)/shard_map/reduce_sum | solution.py:96
  86.2 3.9 %multiply_convert_fusion.2 = (bf16[256,256]{1,0:T(8,128)(2,1)S(1)}, f32[256,256]{1,0:T(8,128)S(1)}) fusion(f32[256,512]{1,0:T(8,128)S(1)} %fusion.98, f32[256]{0:T(256)} %get-tuple-element.172, f32[241,256]{1,0:T(8,128)S(1)} %get-tuple-element.48, f32[256]{0:T(256)} %bitcast.33, f32[256]{0:T(256)} %get-tuple-element.141, ...), kind=kLoop, calls=%fused_computation.51 | loop fusion | flops 6356992 | bytes 8599552 | tf_op jit(solution)/shard_map/convert.1
  91.4 1.9 pad_maximum_fusion
  93.3 3.5 %copy.23 = f32[1024,768]{1,0:T(8,128)} copy(f32[1024,768]{0,1:T(8,128)} %pad_maximum_fusion) | data formatting | bytes 6291456 | tf_op jit(solution)/shard_map/concatenate | solution.py:116
  96.9 2.4 %fusion.3 = bf16[64,8,768]{2,1,0:T(8,128)(2,1)} fusion(f32[64,2,8,768]{3,2,1,0:T(8,128)} %bitcast.101, s32[]{:T(128)S(6)} %select_n.12), kind=kLoop, calls=%fused_computation.11 | loop fusion | bytes 1572868 | tf_op jit(solution)/shard_map/convert_element_type | solution.py:40
  99.3 1.9 collective-permute-start
  101.2 1.4 convolution_convert_fusion
  103.5 4.8 %all-to-all-start.2 = ((bf16[4,256,256]{2,1,0:T(8,128)(2,1)}), bf16[4,256,256]{2,1,0:T(8,128)(2,1)S(1)}, u32[]{:S(2)}, u32[]{:S(2)}) async-start(bf16[4,256,256]{2,1,0:T(8,128)(2,1)} %bitcast.100), calls=%async_computation.2 | async-start | bytes 1048576 | tf_op jit(solution)/shard_map/all_to_all | solution.py:113
  108.3 2.7 %fusion = bf16[64,8,768]{2,1,0:T(8,128)(2,1)} fusion(bf16[64,8,768]{2,1,0:T(8,128)(2,1)} %collective-permute-done, f32[64,2,8,768]{3,2,1,0:T(8,128)} %bitcast.102, s32[]{:T(128)S(6)} %select_n.11), kind=kLoop, calls=%fused_computation.3 | loop fusion | flops 1179648 | bytes 3145732 | tf_op jit(solution)/shard_map/convert_element_type | solution.py:42
  111.0 5.9 %all-to-all-done.2 = bf16[4,256,256]{2,1,0:T(8,128)(2,1)S(1)} async-done(((bf16[4,256,256]{2,1,0:T(8,128)(2,1)}), bf16[4,256,256]{2,1,0:T(8,128)(2,1)S(1)}, u32[]{:S(2)}, u32[]{:S(2)}) %all-to-all-start.2) | async-done | bytes 524320 | tf_op jit(solution)/shard_map/all_to_all | solution.py:113
  117.8 4.8 %all-to-all-start.3 = ((bf16[64,8,768]{2,1,0:T(8,128)(2,1)}), bf16[64,8,768]{2,1,0:T(8,128)(2,1)S(1)}, u32[]{:S(2)}, u32[]{:S(2)}) async-start(bf16[64,8,768]{2,1,0:T(8,128)(2,1)} %fusion), calls=%async_computation.3 | async-start | bytes 1572864 | tf_op jit(solution)/shard_map/all_to_all | solution.py:43
  122.7 2.3 %multiply_reduce_fusion.27 = (f32[256]{0:T(256)}, f32[256]{0:T(256)}, f32[256]{0:T(256)}, f32[256]{0:T(256)}) fusion(f32[256,256]{1,0:T(8,128)S(1)} %get-tuple-element.41, f32[244,256]{1,0:T(8,128)} %copy-done.23, f32[256]{0:T(256)} %get-tuple-element.171, f32[256]{0:T(256)} %get-tuple-element.159, f32[243,256]{1,0:T(8,128)} %copy-done.22, ...), kind=kLoop, calls=%fused_computation.45 | loop fusion | flops 785408 | bytes 1263616 | tf_op jit(solution)/shard_map/reduce_sum | solution.py:96
  125.0 2.5 %multiply_reduce_fusion.18 = (f32[256]{0:T(256)}, f32[256]{0:T(256)}, f32[256]{0:T(256)}, f32[256]{0:T(256)}, f32[256]{0:T(256)}, /*index=5*/f32[256]{0:T(256)}, f32[256]{0:T(256)}, f32[256]{0:T(256)}, f32[256]{0:T(256)}) fusion(f32[256,256]{1,0:T(8,128)S(1)} %get-tuple-element.41, f32[253,256]{1,0:T(8,128)S(1)} %get-tuple-element.101, ...), kind=kLoop, calls=%fused_computation.36 | loop fusion | flops 1767168 | bytes 2575360 | tf_op jit(solution)/shard_map/reduce_sum | solution.py:96
  128.8 2.9 %stack.151 = f32[31,256]{1,0:T(8,128)S(1)} concatenate(f32[1,256]{1,0:T(1,128)} %bitcast.128, f32[1,256]{1,0:T(1,128)} %bitcast.127, f32[1,256]{1,0:T(1,128)} %bitcast.126, f32[1,256]{1,0:T(1,128)} %bitcast.125, f32[1,256]{1,0:T(1,128)} %bitcast.137, f32[1,256]{1,0:T(1,128)} %bitcast.136, f32[1,256]{1,0:T(1,128)} %bitcast.135, f32[1,256]{1,0:T(1,128)} %bitcast.134, ...), dimensions={0} | concatenate | bytes 63488 | tf_op jit(solution)/shard_map/stack | solution.py:98
  131.6 3.4 %psum.37 = f32[31,256]{1,0:T(8,128)S(1)} all-reduce(f32[31,256]{1,0:T(8,128)S(1)} %stack.151), channel_id=1, replica_groups=mesh['y'=8,'z'=8,'core'=2,'mp'=4] {'core'}, use_global_device_ids=true, to_apply=%region_44.45 | all-reduce | flops 7936 | bytes 63488 | tf_op jit(solution)/shard_map/psum | solution.py:98
  135.1 29.8 %psum.38 = f32[31,256]{1,0:T(8,128)S(1)} all-reduce(f32[31,256]{1,0:T(8,128)S(1)} %psum.37), channel_id=1, replica_groups=mesh['y'=8,'z'=8,'core'=2,'mp'=4] {'y'}, use_global_device_ids=true, to_apply=%region_45.46 | all-reduce | flops 7936 | bytes 63488 | tf_op jit(solution)/shard_map/psum | solution.py:98
  164.8 30.2 %psum.39 = f32[31,256]{1,0:T(8,128)} all-reduce(f32[31,256]{1,0:T(8,128)S(1)} %psum.38), channel_id=1, replica_groups=mesh['y'=8,'z'=8,'core'=2,'mp'=4] {'z'}, use_global_device_ids=true, to_apply=%region_46.47 | all-reduce | flops 7936 | bytes 63488 | tf_op jit(solution)/shard_map/psum | solution.py:98
  (216 shorter events, 19.1 us)
Async XLA Ops:
  0.6 5.4 %copy-start = (bf16[256,1024]{1,0:T(8,128)(2,1)S(1)}, bf16[256,1024]{1,0:T(8,128)(2,1)}, u32[]{:S(2)}) copy-start(bf16[256,1024]{1,0:T(8,128)(2,1)} %param.9) | copy-start | bytes 1572868
  7.2 8.0 %copy-start.22 = (f32[243,256]{1,0:T(8,128)}, f32[243,256]{1,0:T(8,128)S(1)}, u32[]{:S(2)}) copy-start(f32[243,256]{1,0:T(8,128)S(1)} %get-tuple-element.81) | copy-start | bytes 746500
  7.2 8.0 %copy-start.30 = (f32[243,256]{1,0:T(8,128)}, f32[243,256]{1,0:T(8,128)S(1)}, u32[]{:S(2)}) copy-start(f32[243,256]{1,0:T(8,128)S(1)} %get-tuple-element.82) | copy-start | bytes 746500
  7.3 7.9 %copy-start.23 = (f32[244,256]{1,0:T(8,128)}, f32[244,256]{1,0:T(8,128)S(1)}, u32[]{:S(2)}) copy-start(f32[244,256]{1,0:T(8,128)S(1)} %get-tuple-element.83) | copy-start | bytes 749572
  7.3 7.9 %copy-start.31 = (f32[244,256]{1,0:T(8,128)}, f32[244,256]{1,0:T(8,128)S(1)}, u32[]{:S(2)}) copy-start(f32[244,256]{1,0:T(8,128)S(1)} %get-tuple-element.84) | copy-start | bytes 749572
  7.4 7.9 %copy-start.24 = (f32[245,256]{1,0:T(8,128)}, f32[245,256]{1,0:T(8,128)S(1)}, u32[]{:S(2)}) copy-start(f32[245,256]{1,0:T(8,128)S(1)} %get-tuple-element.85) | copy-start | bytes 752644
  7.4 7.9 %copy-start.32 = (f32[245,256]{1,0:T(8,128)}, f32[245,256]{1,0:T(8,128)S(1)}, u32[]{:S(2)}) copy-start(f32[245,256]{1,0:T(8,128)S(1)} %get-tuple-element.86) | copy-start | bytes 752644
  7.4 7.9 %copy-start.25 = (f32[246,256]{1,0:T(8,128)}, f32[246,256]{1,0:T(8,128)S(1)}, u32[]{:S(2)}) copy-start(f32[246,256]{1,0:T(8,128)S(1)} %get-tuple-element.87) | copy-start | bytes 755716
  7.4 7.9 %copy-start.33 = (f32[246,256]{1,0:T(8,128)}, f32[246,256]{1,0:T(8,128)S(1)}, u32[]{:S(2)}) copy-start(f32[246,256]{1,0:T(8,128)S(1)} %get-tuple-element.88) | copy-start | bytes 755716
  7.5 7.8 %copy-start.26 = (f32[247,256]{1,0:T(8,128)}, f32[247,256]{1,0:T(8,128)S(1)}, u32[]{:S(2)}) copy-start(f32[247,256]{1,0:T(8,128)S(1)} %get-tuple-element.89) | copy-start | bytes 758788
  7.5 7.8 %copy-start.34 = (f32[247,256]{1,0:T(8,128)}, f32[247,256]{1,0:T(8,128)S(1)}, u32[]{:S(2)}) copy-start(f32[247,256]{1,0:T(8,128)S(1)} %get-tuple-element.90) | copy-start | bytes 758788
  8.0 7.3 %copy-start.27 = (f32[248,256]{1,0:T(8,128)}, f32[248,256]{1,0:T(8,128)S(1)}, u32[]{:S(2)}) copy-start(f32[248,256]{1,0:T(8,128)S(1)} %get-tuple-element.91) | copy-start | bytes 761860
  8.0 7.4 %copy-start.35 = (f32[248,256]{1,0:T(8,128)}, f32[248,256]{1,0:T(8,128)S(1)}, u32[]{:S(2)}) copy-start(f32[248,256]{1,0:T(8,128)S(1)} %get-tuple-element.92) | copy-start | bytes 761860
  15.4 66.6 %copy-start.40 = (f32[256,256]{1,0:T(8,128)}, f32[256,256]{1,0:T(8,128)S(1)}, u32[]{:S(2)}) copy-start(f32[256,256]{1,0:T(8,128)S(1)} %get-tuple-element.46) | copy-start | bytes 786436
  20.6 29.7 %all-to-all-start = ((f32[64,2,256]{2,1,0:T(2,128)}), f32[64,2,256]{2,1,0:T(2,128)}, u32[]{:S(2)}, u32[]{:S(2)}) async-start(f32[64,2,256]{2,1,0:T(2,128)} %broadcast_in_dim.4), calls=%async_computation | async-start | bytes 262144 | tf_op jit(solution)/shard_map/all_to_all | solution.py:31
  60.5 18.7 %all-to-all-start.1 = ((f32[64,2,256]{2,1,0:T(2,128)}), f32[64,2,256]{2,1,0:T(2,128)}, u32[]{:S(2)}, u32[]{:S(2)}) async-start(f32[64,2,256]{2,1,0:T(2,128)} %broadcast_in_dim.5), calls=%async_computation.1 | async-start | bytes 262144 | tf_op jit(solution)/shard_map/all_to_all | solution.py:31
  99.3 9.0 %collective-permute-start = (bf16[64,8,768]{2,1,0:T(8,128)(2,1)}, bf16[64,8,768]{2,1,0:T(8,128)(2,1)}, u32[]{:S(2)}, u32[]{:S(2)}) collective-permute-start(bf16[64,8,768]{2,1,0:T(8,128)(2,1)} %fusion.3), channel_id=1, source_target_pairs={{0,4},{4,0},{1,5},{5,1},{2,6},{6,2},{3,7},{7,3},{8,12},{12,8},{9,1... | collective-permute-start | bytes 2359304 | tf_op jit(solution)/shard_map/ppermute | solution.py:41
  103.5 13.5 %all-to-all-start.2 = ((bf16[4,256,256]{2,1,0:T(8,128)(2,1)}), bf16[4,256,256]{2,1,0:T(8,128)(2,1)S(1)}, u32[]{:S(2)}, u32[]{:S(2)}) async-start(bf16[4,256,256]{2,1,0:T(8,128)(2,1)} %bitcast.100), calls=%async_computation.2 | async-start | bytes 1048576 | tf_op jit(solution)/shard_map/all_to_all | solution.py:113
  108.3 16.7 %copy-start.2 = (f32[251,256]{1,0:T(8,128)S(1)}, f32[251,256]{1,0:T(8,128)}, u32[]{:S(2)}) copy-start(f32[251,256]{1,0:T(8,128)} %copy-done.1) | copy-start | bytes 771076
  108.3 16.7 %copy-start.63 = (f32[256]{0:T(256)S(1)}, f32[256]{0:T(256)}, u32[]{:S(2)}) copy-start(f32[256]{0:T(256)} %copy-done.61) | copy-start | bytes 3076
  111.0 16.5 %copy-start.5 = (f32[252,256]{1,0:T(8,128)S(1)}, f32[252,256]{1,0:T(8,128)}, u32[]{:S(2)}) copy-start(f32[252,256]{1,0:T(8,128)} %copy-done.4) | copy-start | bytes 774148
  111.0 16.5 %copy-start.7 = (f32[253,256]{1,0:T(8,128)S(1)}, f32[253,256]{1,0:T(8,128)}, u32[]{:S(2)}) copy-start(f32[253,256]{1,0:T(8,128)} %copy-done.6) | copy-start | bytes 777220
  111.0 16.5 %copy-start.57 = (f32[256]{0:T(256)S(1)}, f32[256]{0:T(256)}, u32[]{:S(2)}) copy-start(f32[256]{0:T(256)} %copy-done.55) | copy-start | bytes 3076
  111.0 16.5 %copy-start.60 = (f32[256]{0:T(256)S(1)}, f32[256]{0:T(256)}, u32[]{:S(2)}) copy-start(f32[256]{0:T(256)} %copy-done.58) | copy-start | bytes 3076
  117.8 78.0 %all-to-all-start.3 = ((bf16[64,8,768]{2,1,0:T(8,128)(2,1)}), bf16[64,8,768]{2,1,0:T(8,128)(2,1)S(1)}, u32[]{:S(2)}, u32[]{:S(2)}) async-start(bf16[64,8,768]{2,1,0:T(8,128)(2,1)} %fusion), calls=%async_computation.3 | async-start | bytes 1572864 | tf_op jit(solution)/shard_map/all_to_all | solution.py:43
  122.6 4.9 %copy-start.9 = (f32[254,256]{1,0:T(8,128)S(1)}, f32[254,256]{1,0:T(8,128)}, u32[]{:S(2)}) copy-start(f32[254,256]{1,0:T(8,128)} %copy-done.8) | copy-start | bytes 780292
  122.6 4.9 %copy-start.11 = (f32[254,256]{1,0:T(8,128)S(1)}, f32[254,256]{1,0:T(8,128)}, u32[]{:S(2)}) copy-start(f32[254,256]{1,0:T(8,128)} %copy-done.10) | copy-start | bytes 780292
  122.6 4.9 %copy-start.13 = (f32[255,256]{1,0:T(8,128)S(1)}, f32[255,256]{1,0:T(8,128)}, u32[]{:S(2)}) copy-start(f32[255,256]{1,0:T(8,128)} %copy-done.12) | copy-start | bytes 783364
  122.6 4.9 %copy-start.15 = (f32[255,256]{1,0:T(8,128)S(1)}, f32[255,256]{1,0:T(8,128)}, u32[]{:S(2)}) copy-start(f32[255,256]{1,0:T(8,128)} %copy-done.14) | copy-start | bytes 783364
  122.6 4.9 %copy-start.17 = (f32[250,256]{1,0:T(8,128)S(1)}, f32[250,256]{1,0:T(8,128)}, u32[]{:S(2)}) copy-start(f32[250,256]{1,0:T(8,128)} %copy-done.16) | copy-start | bytes 768004
  122.6 4.9 %copy-start.19 = (f32[251,256]{1,0:T(8,128)S(1)}, f32[251,256]{1,0:T(8,128)}, u32[]{:S(2)}) copy-start(f32[251,256]{1,0:T(8,128)} %copy-done.18) | copy-start | bytes 771076
  127.6 67.5 %copy-start.37 = (bf16[4,256,256]{2,1,0:T(8,128)(2,1)S(1)}, bf16[4,256,256]{2,1,0:T(8,128)(2,1)}, u32[]{:S(2)}) copy-start(bf16[4,256,256]{2,1,0:T(8,128)(2,1)} %copy-done.36) | copy-start | bytes 1572868
  (46 other events, 134.1 us)
where the time goes:
time: 198 us; the launch traced here: 197 us
  blocking collectives  69.7 us (35%)
  starting transfers between devices  33.9 us (17%)
  other arithmetic  32.5 us (16%)
  waiting for transfers between devices  27.5 us (14%)
  local copies, waits for them, and re-layouts  23.4 us (12%)
  matrix products  7.04 us (4%)
  between operations  3.18 us (2%)
    psum x1, blocking collectives, shards(): lax.psum(lax.psum(lax.psum(jnp.stack(depth_rows), 'core'), 'y'), 'z')  30.2 us
    psum x1, blocking collectives, shards(): lax.psum(lax.psum(jnp.stack(depth_rows), 'core'), 'y')  29.8 us
    all_to_all x2, starting transfers between devices, small_sum(): return jnp.sum(lax.all_to_all(every, ('y', 'z'), 0, 0), axis=0)  22.3 us
    all_to_all x2, waiting for transfers between devices, small_sum(): return jnp.sum(lax.all_to_all(every, ('y', 'z'), 0, 0), axis=0)  21.6 us
    reduce_sum x4, other arithmetic, shards(): jnp.sum(grad_conv * tap_term(glu_float, owner_id, live_col, tap_index - r...  8.92 us
    psum x2, blocking collectives, small_sum(): x = lax.psum(x, 'core')  6.29 us
    all_to_all x1, waiting for transfers between devices, shards(): frame_parts = lax.all_to_all(jnp.swapaxes(frame_parts, 0, 1), 'mp', 0, 0)  5.93 us
    another operation x3, other arithmetic  4.9 us
  transfers between devices with their start and end apart: 5, of which 3 were waited for; matrix products, arithmetic and copies ran while one was open for 9% of the time, Pallas kernels for 0%

commit v1 on v0

--- a/solution.py
+++ b/solution.py
@@ -95,7 +95,9 @@
         depth_rows.append(
             jnp.sum(grad_conv * tap_term(glu_float, owner_id, live_col, tap_index - radius), axis=0)
         )
-    depth_grad = lax.psum(lax.psum(lax.psum(jnp.stack(depth_rows), "core"), "y"), "z")
+    depth_grad = lax.psum(
+        lax.psum(jnp.sum(lax.all_gather(jnp.stack(depth_rows), "core"), axis=0), "y"), "z"
+    )
     grad_glu = jnp.zeros((frames_dev, channels), jnp.float32)
     for tap_index in range(tap_count):
         offset = tap_index - radius

time: 198 us -> 198 us (level)
    psum x3 -> x2, blocking collectives: 63.4 us -> 60.8 us  [the longest x1 30.6 us: shards(): lax.psum(jnp.sum(lax.all_gather(jnp.stack(depth_rows), 'core'), axis=0),...]
where the time goes in v1:
time: 198 us; the launch traced here: 196 us
  blocking collectives  69 us (35%)
  starting transfers between devices  33.7 us (17%)
  other arithmetic  32.5 us (16%)
  waiting for transfers between devices  27.5 us (14%)
  local copies, waits for them, and re-layouts  23.4 us (12%)
  matrix products  7.04 us (4%)
  between operations  3.17 us (2%)
    psum x1, blocking collectives, shards(): lax.psum(jnp.sum(lax.all_gather(jnp.stack(depth_rows), 'core'), axis=0),...  30.6 us
    psum x1, blocking collectives, shards(): lax.psum(lax.psum(jnp.sum(lax.all_gather(jnp.stack(depth_rows), 'core'),...  30.2 us
    all_to_all x2, starting transfers between devices, small_sum(): return jnp.sum(lax.all_to_all(every, ('y', 'z'), 0, 0), axis=0)  22.3 us
    all_to_all x2, waiting for transfers between devices, small_sum(): return jnp.sum(lax.all_to_all(every, ('y', 'z'), 0, 0), axis=0)  21.6 us
    reduce_sum x4, other arithmetic, shards(): jnp.sum(grad_conv * tap_term(glu_float, owner_id, live_col, tap_index - r...  8.92 us
    psum x2, blocking collectives, small_sum(): x = lax.psum(x, 'core')  6.29 us
    all_to_all x1, waiting for transfers between devices, shards(): frame_parts = lax.all_to_all(jnp.swapaxes(frame_parts, 0, 1), 'mp', 0, 0)  5.93 us
    another operation x3, other arithmetic  4.9 us
  transfers between devices with their start and end apart: 5, of which 3 were waited for; matrix products, arithmetic and copies ran while one was open for 9% of the time, Pallas kernels for 0%

profile of v1, /device:TPU:2, one launch (start us, length us, event | category | flops | bytes accessed | tf_op | source)
XLA Modules:
  0.0 196.3 jit_solution(1570528652343166006)
XLA Ops:
  4.6 1.5 copy.31
  11.3 3.9 %fusion.49 = (f32[256]{0:T(256)S(1)}, f32[256]{0:T(256)S(1)}, f32[256,256]{1,0:T(8,128)S(1)}) fusion(f32[256]{0:T(256)S(1)} %get-tuple-element.142, f32[241,256]{1,0:T(8,128)S(1)} %get-tuple-element.78, f32[256]{0:T(256)} %bitcast.33, f32[256]{0:T(256)S(1)} %get-tuple-element.143, f32[242,256]{1,0:T(8,128)S(1)} %get-tuple-element.80, f32[256]{0:T(256)} %bitcast.32, ...), kind=kLoop, calls=%fused_computation.171 | loop fusion | flops 6290944 | bytes 8077312 | tf_op jit(solution)/shard_map/reduce_sum | solution.py:73
  16.1 3.1 %psum.28 = f32[2,256]{1,0:T(2,128)} all-reduce(f32[2,256]{1,0:T(2,128)} %pad_maximum_fusion.4), channel_id=1, replica_groups=mesh['y'=8,'z'=8,'core'=2,'mp'=4] {'core'}, use_global_device_ids=true, to_apply=%region_4.5 | all-reduce | flops 512 | bytes 4096 | tf_op jit(solution)/shard_map/psum | solution.py:28
  19.2 1.4 broadcast_in_dim.4
  20.6 16.9 %all-to-all-start = ((f32[64,2,256]{2,1,0:T(2,128)}), f32[64,2,256]{2,1,0:T(2,128)}, u32[]{:S(2)}, u32[]{:S(2)}) async-start(f32[64,2,256]{2,1,0:T(2,128)} %broadcast_in_dim.4), calls=%async_computation | async-start | bytes 262144 | tf_op jit(solution)/shard_map/all_to_all | solution.py:31
  39.4 10.9 %all-to-all-done = f32[64,2,256]{2,1,0:T(2,128)} async-done(((f32[64,2,256]{2,1,0:T(2,128)}), f32[64,2,256]{2,1,0:T(2,128)}, u32[]{:S(2)}, u32[]{:S(2)}) %all-to-all-start) | async-done | bytes 131104 | tf_op jit(solution)/shard_map/all_to_all | solution.py:31
  50.3 1.6 reduce_sum.384
  53.2 2.2 %fusion.48 = (f32[256]{0:T(256)S(1)}, f32[256]{0:T(256)S(1)}, f32[256,256]{1,0:T(8,128)}) fusion(f32[256]{0:T(256)S(1)} %bitcast.120, f32[256,256]{1,0:T(8,128)S(1)} %get-tuple-element.46, f32[256]{0:T(256)S(1)} %bitcast.123, f32[256]{0:T(256)} %param.13, f32[256]{0:T(256)} %param.12, f32[256]{0:T(256)S(1)} %fusion.44, bf16[256,1024]{1,0:T(8,128)(2,1)} %param.15, ...), kind=kOutput, calls=%fused_computation.170 | convolution fusion | flops 135265792 | bytes 1580032 | tf_op jit(solution)/shard_map/dot_general | solution.py:82
  56.0 3.1 %psum.29 = f32[2,256]{1,0:T(2,128)} all-reduce(f32[2,256]{1,0:T(2,128)} %pad_maximum_fusion.5), channel_id=1, replica_groups=mesh['y'=8,'z'=8,'core'=2,'mp'=4] {'core'}, use_global_device_ids=true, to_apply=%region_9.10 | all-reduce | flops 512 | bytes 4096 | tf_op jit(solution)/shard_map/psum | solution.py:28
  59.2 1.4 broadcast_in_dim.5
  60.5 5.4 %all-to-all-start.1 = ((f32[64,2,256]{2,1,0:T(2,128)}), f32[64,2,256]{2,1,0:T(2,128)}, u32[]{:S(2)}, u32[]{:S(2)}) async-start(f32[64,2,256]{2,1,0:T(2,128)} %broadcast_in_dim.5), calls=%async_computation.1 | async-start | bytes 262144 | tf_op jit(solution)/shard_map/all_to_all | solution.py:31
  66.0 2.5 %convolution_bitcast_fusion.1 = f32[1024,256]{0,1:T(8,128)} fusion(bf16[256,1024]{1,0:T(8,128)(2,1)} %param.15, f32[256,256]{1,0:T(8,128)S(1)} %get-tuple-element.46, f32[256]{0:T(256)} %param.13, f32[256]{0:T(256)} %bitcast.124, f32[256]{0:T(256)} %bitcast.121, f32[256]{0:T(256)} %param.12, f32[256]{0:T(256)S(1)} %fusion.44), kind=kOutput, calls=%fused_computation.6 | convolution fusion | flops 134873088 | bytes 1840128 | tf_op jit(solution)/shard_map/dot_general | solution.py:123
  68.5 10.7 %all-to-all-done.1 = f32[64,2,256]{2,1,0:T(2,128)} async-done(((f32[64,2,256]{2,1,0:T(2,128)}), f32[64,2,256]{2,1,0:T(2,128)}, u32[]{:S(2)}, u32[]{:S(2)}) %all-to-all-start.1) | async-done | bytes 131104 | tf_op jit(solution)/shard_map/all_to_all | solution.py:31
  79.2 1.6 reduce_sum.388
  80.8 1.3 fusion.82
  82.1 2.9 %multiply_reduce_fusion = (f32[256]{0:T(256)}, f32[256]{0:T(256)}, f32[256]{0:T(256)}, f32[256]{0:T(256)}, f32[256]{0:T(256)}, /*index=5*/f32[256]{0:T(256)}, f3...) fusion(f32[241,256]{1,0:T(8,128)} %copy-done.28, f32[256]{0:T(256)S(1)} %get-tuple-element.142, ...), kind=kLoop, calls=%fused_computation.18 | loop fusion | flops 2356992 | bytes 3068932 | tf_op jit(solution)/shard_map/reduce_sum | solution.py:96
  86.2 3.9 %multiply_convert_fusion.2 = (bf16[256,256]{1,0:T(8,128)(2,1)S(1)}, f32[256,256]{1,0:T(8,128)S(1)}) fusion(f32[256,512]{1,0:T(8,128)S(1)} %fusion.98, f32[256]{0:T(256)} %get-tuple-element.172, f32[241,256]{1,0:T(8,128)S(1)} %get-tuple-element.48, f32[256]{0:T(256)} %bitcast.33, f32[256]{0:T(256)} %get-tuple-element.141, ...), kind=kLoop, calls=%fused_computation.51 | loop fusion | flops 6356992 | bytes 8599552 | tf_op jit(solution)/shard_map/convert.1
  91.4 1.9 pad_maximum_fusion
  93.3 3.5 %copy.23 = f32[1024,768]{1,0:T(8,128)} copy(f32[1024,768]{0,1:T(8,128)} %pad_maximum_fusion) | data formatting | bytes 6291456 | tf_op jit(solution)/shard_map/concatenate | solution.py:118
  96.9 2.4 %fusion.3 = bf16[64,8,768]{2,1,0:T(8,128)(2,1)} fusion(f32[64,2,8,768]{3,2,1,0:T(8,128)} %bitcast.102, s32[]{:T(128)S(6)} %select_n.12), kind=kLoop, calls=%fused_computation.11 | loop fusion | bytes 1572868 | tf_op jit(solution)/shard_map/convert_element_type | solution.py:40
  99.3 1.9 collective-permute-start
  101.2 1.4 convolution_convert_fusion
  103.5 4.8 %all-to-all-start.2 = ((bf16[4,256,256]{2,1,0:T(8,128)(2,1)}), bf16[4,256,256]{2,1,0:T(8,128)(2,1)S(1)}, u32[]{:S(2)}, u32[]{:S(2)}) async-start(bf16[4,256,256]{2,1,0:T(8,128)(2,1)} %bitcast.101), calls=%async_computation.2 | async-start | bytes 1048576 | tf_op jit(solution)/shard_map/all_to_all | solution.py:115
  108.3 2.7 %fusion = bf16[64,8,768]{2,1,0:T(8,128)(2,1)} fusion(bf16[64,8,768]{2,1,0:T(8,128)(2,1)} %collective-permute-done, f32[64,2,8,768]{3,2,1,0:T(8,128)} %bitcast.103, s32[]{:T(128)S(6)} %select_n.11), kind=kLoop, calls=%fused_computation.3 | loop fusion | flops 1179648 | bytes 3145732 | tf_op jit(solution)/shard_map/convert_element_type | solution.py:42
  111.0 5.9 %all-to-all-done.2 = bf16[4,256,256]{2,1,0:T(8,128)(2,1)S(1)} async-done(((bf16[4,256,256]{2,1,0:T(8,128)(2,1)}), bf16[4,256,256]{2,1,0:T(8,128)(2,1)S(1)}, u32[]{:S(2)}, u32[]{:S(2)}) %all-to-all-start.2) | async-done | bytes 524320 | tf_op jit(solution)/shard_map/all_to_all | solution.py:115
  117.8 4.6 %all-to-all-start.3 = ((bf16[64,8,768]{2,1,0:T(8,128)(2,1)}), bf16[64,8,768]{2,1,0:T(8,128)(2,1)S(1)}, u32[]{:S(2)}, u32[]{:S(2)}) async-start(bf16[64,8,768]{2,1,0:T(8,128)(2,1)} %fusion), calls=%async_computation.3 | async-start | bytes 1572864 | tf_op jit(solution)/shard_map/all_to_all | solution.py:43
  122.5 2.3 %multiply_reduce_fusion.27 = (f32[256]{0:T(256)}, f32[256]{0:T(256)}, f32[256]{0:T(256)}, f32[256]{0:T(256)}) fusion(f32[256,256]{1,0:T(8,128)S(1)} %get-tuple-element.41, f32[244,256]{1,0:T(8,128)} %copy-done.23, f32[256]{0:T(256)} %get-tuple-element.171, f32[256]{0:T(256)} %get-tuple-element.159, f32[243,256]{1,0:T(8,128)} %copy-done.22, ...), kind=kLoop, calls=%fused_computation.45 | loop fusion | flops 785408 | bytes 1263616 | tf_op jit(solution)/shard_map/reduce_sum | solution.py:96
  124.8 2.5 %multiply_reduce_fusion.18 = (f32[256]{0:T(256)}, f32[256]{0:T(256)}, f32[256]{0:T(256)}, f32[256]{0:T(256)}, f32[256]{0:T(256)}, /*index=5*/f32[256]{0:T(256)}, f32[256]{0:T(256)}, f32[256]{0:T(256)}, f32[256]{0:T(256)}) fusion(f32[256,256]{1,0:T(8,128)S(1)} %get-tuple-element.41, f32[253,256]{1,0:T(8,128)S(1)} %get-tuple-element.101, ...), kind=kLoop, calls=%fused_computation.36 | loop fusion | flops 1767168 | bytes 2575360 | tf_op jit(solution)/shard_map/reduce_sum | solution.py:96
  128.6 2.9 %stack.151 = f32[31,256]{1,0:T(8,128)S(1)} concatenate(f32[1,256]{1,0:T(1,128)} %bitcast.130, f32[1,256]{1,0:T(1,128)} %bitcast.129, f32[1,256]{1,0:T(1,128)} %bitcast.128, f32[1,256]{1,0:T(1,128)} %bitcast.127, f32[1,256]{1,0:T(1,128)} %bitcast.139, f32[1,256]{1,0:T(1,128)} %bitcast.138, f32[1,256]{1,0:T(1,128)} %bitcast.137, f32[1,256]{1,0:T(1,128)} %bitcast.136, ...), dimensions={0} | concatenate | bytes 63488 | tf_op jit(solution)/shard_map/stack | solution.py:99
  131.5 1.9 all-gather.1
  133.3 30.6 %psum.30 = f32[31,256]{1,0:T(8,128)S(1)} all-reduce(f32[31,256]{1,0:T(8,128)S(1)} %reduce_sum.422), channel_id=1, replica_groups=mesh['y'=8,'z'=8,'core'=2,'mp'=4] {'y'}, use_global_device_ids=true, to_apply=%region_45.46 | all-reduce | flops 7936 | bytes 63488 | tf_op jit(solution)/shard_map/psum | solution.py:99
  163.9 30.2 %psum.31 = f32[31,256]{1,0:T(8,128)} all-reduce(f32[31,256]{1,0:T(8,128)S(1)} %psum.30), channel_id=1, replica_groups=mesh['y'=8,'z'=8,'core'=2,'mp'=4] {'z'}, use_global_device_ids=true, to_apply=%region_46.47 | all-reduce | flops 7936 | bytes 63488 | tf_op jit(solution)/shard_map/psum | solution.py:98
  (217 shorter events, 19.2 us)
Async XLA Ops:
  0.6 5.4 %copy-start = (bf16[256,1024]{1,0:T(8,128)(2,1)S(1)}, bf16[256,1024]{1,0:T(8,128)(2,1)}, u32[]{:S(2)}) copy-start(bf16[256,1024]{1,0:T(8,128)(2,1)} %param.9) | copy-start | bytes 1572868
  7.2 8.0 %copy-start.22 = (f32[243,256]{1,0:T(8,128)}, f32[243,256]{1,0:T(8,128)S(1)}, u32[]{:S(2)}) copy-start(f32[243,256]{1,0:T(8,128)S(1)} %get-tuple-element.81) | copy-start | bytes 746500
  7.2 8.0 %copy-start.30 = (f32[243,256]{1,0:T(8,128)}, f32[243,256]{1,0:T(8,128)S(1)}, u32[]{:S(2)}) copy-start(f32[243,256]{1,0:T(8,128)S(1)} %get-tuple-element.82) | copy-start | bytes 746500
  7.3 7.9 %copy-start.23 = (f32[244,256]{1,0:T(8,128)}, f32[244,256]{1,0:T(8,128)S(1)}, u32[]{:S(2)}) copy-start(f32[244,256]{1,0:T(8,128)S(1)} %get-tuple-element.83) | copy-start | bytes 749572
  7.3 7.9 %copy-start.31 = (f32[244,256]{1,0:T(8,128)}, f32[244,256]{1,0:T(8,128)S(1)}, u32[]{:S(2)}) copy-start(f32[244,256]{1,0:T(8,128)S(1)} %get-tuple-element.84) | copy-start | bytes 749572
  7.3 7.9 %copy-start.24 = (f32[245,256]{1,0:T(8,128)}, f32[245,256]{1,0:T(8,128)S(1)}, u32[]{:S(2)}) copy-start(f32[245,256]{1,0:T(8,128)S(1)} %get-tuple-element.85) | copy-start | bytes 752644
  7.4 7.9 %copy-start.32 = (f32[245,256]{1,0:T(8,128)}, f32[245,256]{1,0:T(8,128)S(1)}, u32[]{:S(2)}) copy-start(f32[245,256]{1,0:T(8,128)S(1)} %get-tuple-element.86) | copy-start | bytes 752644
  7.4 7.9 %copy-start.25 = (f32[246,256]{1,0:T(8,128)}, f32[246,256]{1,0:T(8,128)S(1)}, u32[]{:S(2)}) copy-start(f32[246,256]{1,0:T(8,128)S(1)} %get-tuple-element.87) | copy-start | bytes 755716
  7.4 7.9 %copy-start.33 = (f32[246,256]{1,0:T(8,128)}, f32[246,256]{1,0:T(8,128)S(1)}, u32[]{:S(2)}) copy-start(f32[246,256]{1,0:T(8,128)S(1)} %get-tuple-element.88) | copy-start | bytes 755716
  7.5 7.8 %copy-start.26 = (f32[247,256]{1,0:T(8,128)}, f32[247,256]{1,0:T(8,128)S(1)}, u32[]{:S(2)}) copy-start(f32[247,256]{1,0:T(8,128)S(1)} %get-tuple-element.89) | copy-start | bytes 758788
  7.5 7.8 %copy-start.34 = (f32[247,256]{1,0:T(8,128)}, f32[247,256]{1,0:T(8,128)S(1)}, u32[]{:S(2)}) copy-start(f32[247,256]{1,0:T(8,128)S(1)} %get-tuple-element.90) | copy-start | bytes 758788
  8.0 7.3 %copy-start.27 = (f32[248,256]{1,0:T(8,128)}, f32[248,256]{1,0:T(8,128)S(1)}, u32[]{:S(2)}) copy-start(f32[248,256]{1,0:T(8,128)S(1)} %get-tuple-element.91) | copy-start | bytes 761860
  8.0 7.4 %copy-start.35 = (f32[248,256]{1,0:T(8,128)}, f32[248,256]{1,0:T(8,128)S(1)}, u32[]{:S(2)}) copy-start(f32[248,256]{1,0:T(8,128)S(1)} %get-tuple-element.92) | copy-start | bytes 761860
  15.4 66.6 %copy-start.40 = (f32[256,256]{1,0:T(8,128)}, f32[256,256]{1,0:T(8,128)S(1)}, u32[]{:S(2)}) copy-start(f32[256,256]{1,0:T(8,128)S(1)} %get-tuple-element.46) | copy-start | bytes 786436
  20.6 29.7 %all-to-all-start = ((f32[64,2,256]{2,1,0:T(2,128)}), f32[64,2,256]{2,1,0:T(2,128)}, u32[]{:S(2)}, u32[]{:S(2)}) async-start(f32[64,2,256]{2,1,0:T(2,128)} %broadcast_in_dim.4), calls=%async_computation | async-start | bytes 262144 | tf_op jit(solution)/shard_map/all_to_all | solution.py:31
  60.5 18.7 %all-to-all-start.1 = ((f32[64,2,256]{2,1,0:T(2,128)}), f32[64,2,256]{2,1,0:T(2,128)}, u32[]{:S(2)}, u32[]{:S(2)}) async-start(f32[64,2,256]{2,1,0:T(2,128)} %broadcast_in_dim.5), calls=%async_computation.1 | async-start | bytes 262144 | tf_op jit(solution)/shard_map/all_to_all | solution.py:31
  99.3 9.0 %collective-permute-start = (bf16[64,8,768]{2,1,0:T(8,128)(2,1)}, bf16[64,8,768]{2,1,0:T(8,128)(2,1)}, u32[]{:S(2)}, u32[]{:S(2)}) collective-permute-start(bf16[64,8,768]{2,1,0:T(8,128)(2,1)} %fusion.3), channel_id=1, source_target_pairs={{0,4},{4,0},{1,5},{5,1},{2,6},{6,2},{3,7},{7,3},{8,12},{12,8},{9,1... | collective-permute-start | bytes 2359304 | tf_op jit(solution)/shard_map/ppermute | solution.py:41
  103.5 13.5 %all-to-all-start.2 = ((bf16[4,256,256]{2,1,0:T(8,128)(2,1)}), bf16[4,256,256]{2,1,0:T(8,128)(2,1)S(1)}, u32[]{:S(2)}, u32[]{:S(2)}) async-start(bf16[4,256,256]{2,1,0:T(8,128)(2,1)} %bitcast.101), calls=%async_computation.2 | async-start | bytes 1048576 | tf_op jit(solution)/shard_map/all_to_all | solution.py:115
  108.3 16.5 %copy-start.2 = (f32[251,256]{1,0:T(8,128)S(1)}, f32[251,256]{1,0:T(8,128)}, u32[]{:S(2)}) copy-start(f32[251,256]{1,0:T(8,128)} %copy-done.1) | copy-start | bytes 771076
  108.3 16.5 %copy-start.63 = (f32[256]{0:T(256)S(1)}, f32[256]{0:T(256)}, u32[]{:S(2)}) copy-start(f32[256]{0:T(256)} %copy-done.61) | copy-start | bytes 3076
  111.0 16.3 %copy-start.5 = (f32[252,256]{1,0:T(8,128)S(1)}, f32[252,256]{1,0:T(8,128)}, u32[]{:S(2)}) copy-start(f32[252,256]{1,0:T(8,128)} %copy-done.4) | copy-start | bytes 774148
  111.0 16.3 %copy-start.7 = (f32[253,256]{1,0:T(8,128)S(1)}, f32[253,256]{1,0:T(8,128)}, u32[]{:S(2)}) copy-start(f32[253,256]{1,0:T(8,128)} %copy-done.6) | copy-start | bytes 777220
  111.0 16.3 %copy-start.57 = (f32[256]{0:T(256)S(1)}, f32[256]{0:T(256)}, u32[]{:S(2)}) copy-start(f32[256]{0:T(256)} %copy-done.55) | copy-start | bytes 3076
  111.0 16.3 %copy-start.60 = (f32[256]{0:T(256)S(1)}, f32[256]{0:T(256)}, u32[]{:S(2)}) copy-start(f32[256]{0:T(256)} %copy-done.58) | copy-start | bytes 3076
  117.8 77.2 %all-to-all-start.3 = ((bf16[64,8,768]{2,1,0:T(8,128)(2,1)}), bf16[64,8,768]{2,1,0:T(8,128)(2,1)S(1)}, u32[]{:S(2)}, u32[]{:S(2)}) async-start(bf16[64,8,768]{2,1,0:T(8,128)(2,1)} %fusion), calls=%async_computation.3 | async-start | bytes 1572864 | tf_op jit(solution)/shard_map/all_to_all | solution.py:43
  122.4 4.9 %copy-start.9 = (f32[254,256]{1,0:T(8,128)S(1)}, f32[254,256]{1,0:T(8,128)}, u32[]{:S(2)}) copy-start(f32[254,256]{1,0:T(8,128)} %copy-done.8) | copy-start | bytes 780292
  122.4 4.9 %copy-start.11 = (f32[254,256]{1,0:T(8,128)S(1)}, f32[254,256]{1,0:T(8,128)}, u32[]{:S(2)}) copy-start(f32[254,256]{1,0:T(8,128)} %copy-done.10) | copy-start | bytes 780292
  122.4 4.9 %copy-start.13 = (f32[255,256]{1,0:T(8,128)S(1)}, f32[255,256]{1,0:T(8,128)}, u32[]{:S(2)}) copy-start(f32[255,256]{1,0:T(8,128)} %copy-done.12) | copy-start | bytes 783364
  122.4 4.9 %copy-start.15 = (f32[255,256]{1,0:T(8,128)S(1)}, f32[255,256]{1,0:T(8,128)}, u32[]{:S(2)}) copy-start(f32[255,256]{1,0:T(8,128)} %copy-done.14) | copy-start | bytes 783364
  122.5 4.9 %copy-start.17 = (f32[250,256]{1,0:T(8,128)S(1)}, f32[250,256]{1,0:T(8,128)}, u32[]{:S(2)}) copy-start(f32[250,256]{1,0:T(8,128)} %copy-done.16) | copy-start | bytes 768004
  122.5 4.9 %copy-start.19 = (f32[251,256]{1,0:T(8,128)S(1)}, f32[251,256]{1,0:T(8,128)}, u32[]{:S(2)}) copy-start(f32[251,256]{1,0:T(8,128)} %copy-done.18) | copy-start | bytes 771076
  127.4 66.8 %copy-start.37 = (bf16[4,256,256]{2,1,0:T(8,128)(2,1)S(1)}, bf16[4,256,256]{2,1,0:T(8,128)(2,1)}, u32[]{:S(2)}) copy-start(bf16[4,256,256]{2,1,0:T(8,128)(2,1)} %copy-done.36) | copy-start | bytes 1572868
  (46 other events, 134.1 us)
